TPU v7x, 32 devices: a whole 2x2x4 slice. The times are simulated.
32 devices in a mesh: tensor: 4 (over z), context: 4 (over y, core), dp: 2 (over x).
Axes of the slice: x: 2, y: 2, z: 4, core: 2. Of those that a mesh axis runs over, the one named last changes fastest.
Arguments:
- inputs: bfloat16 [2, 3072, 768], P('dp', ('context', 'tensor')), may hold values from -6 to 6
- first_gain: float32 [768], replicated, may hold values from 0.5 to 1.5
- first_shift: float32 [768], replicated, may hold values from -1 to 1
- project_weight: bfloat16 [3, 768, 768], P(None, None, 'tensor'), may hold values from -0.21875 to 0.21875
- project_bias: float32 [2, 768], P(None, 'tensor'), may hold values from -1.5 to 1.5
- attend_weight: bfloat16 [768, 768], P('tensor'), may hold values from -1.25 to 1.25
- attend_bias: float32 [768], replicated, may hold values from -1.5 to 1.5
- second_gain: float32 [768], replicated, may hold values from 0.5 to 1.5
- second_shift: float32 [768], replicated, may hold values from -1 to 1
- expand_weight: bfloat16 [768, 3072], P(None, 'tensor'), may hold values from -0.21875 to 0.21875
- expand_bias: float32 [3072], P('tensor'), may hold values from -1.5 to 1.5
- shrink_weight: bfloat16 [3072, 768], P('tensor'), may hold values from -0.109375 to 0.109375
- shrink_bias: float32 [768], replicated, may hold values from -1.5 to 1.5
- segments: int32 [2, 3072], P('dp'), may hold values from 0 to 15, never falling along the last dimension, each value on 1 to 1536 neighbouring positions
- block_order: int32 [8], replicated, may hold values from 0 to 7, each once
- cotangent: bfloat16 [2, 3072, 768], P('dp', ('context', 'tensor')), may hold values from -6 to 6
Outputs:
- outputs: bfloat16 [2, 3072, 768], P('dp', ('context', 'tensor'))
- grad_inputs: bfloat16 [2, 3072, 768], P('dp', ('context', 'tensor'))
- grad_first_gain: float32 [768], replicated
- grad_first_shift: float32 [768], replicated
- grad_project_weight: float32 [3, 768, 768], P(None, None, 'tensor')
- grad_project_bias: float32 [2, 768], P(None, 'tensor')
- grad_attend_weight: float32 [768, 768], P('tensor')
- grad_attend_bias: float32 [768], replicated
- grad_second_gain: float32 [768], replicated
- grad_second_shift: float32 [768], replicated
- grad_expand_weight: float32 [768, 3072], P(None, 'tensor')
- grad_expand_bias: float32 [3072], P('tensor')
- grad_shrink_weight: float32 [3072, 768], P('tensor')
- grad_shrink_bias: float32 [768], replicated
Inputs may be any that keep to these rules, and one draw needn't show every extreme that they name: `segments`: in each sequence the document numbers never fall; every number appears, each document has 1 to 1536 tokens and one has exactly 1536. Each value appears once: stored block b of 384 tokens holds natural block block_order[b].
All inputs are finite; a program needn't handle non-finite values.
Results may differ from a plain program's by a relative error of at most 0.02.
Values may be sent and summed in bfloat16 or wider, within the bound.
A program may use at most 128 MiB of HBM per device.

v0:
```python
import jax
import jax.numpy as jnp
from jax import lax
from jax.sharding import PartitionSpec as P

HEAD_DIM = 64
NEG_FILL = -1e30
NORM_EPS = 1e-05


def layer_norm(values):
    centre = jnp.mean(values, axis=-1, keepdims=True)
    shifted = values - centre
    spread = jnp.mean(shifted * shifted, axis=-1, keepdims=True)
    return shifted * lax.rsqrt(spread + NORM_EPS)


def affine_norm(values, gain, shift):
    return layer_norm(values) * gain + shift


def gelu_tanh(values):
    return jax.nn.gelu(values, approximate=True)


def stored_places(order, half_rows, seq_len):
    index = jnp.arange(seq_len, dtype=jnp.int32)
    slots = jnp.arange(order.shape[0], dtype=jnp.int32)
    chosen = jnp.sum(
        jnp.where((index // half_rows)[:, None] == slots[None, :], order[None, :], 0), axis=1
    )
    return chosen * half_rows + index % half_rows


def allowed_pairs(query_place, query_seg, key_place, key_seg):
    return (query_seg[:, None] == key_seg[None, :]) & (key_place[None, :] <= query_place[:, None])


def split_heads(values):
    return values.reshape(values.shape[0], -1, HEAD_DIM)


def cross_rows(left, right):
    return lax.dot_general(
        left, right, (((0,), (0,)), ((), ())), preferred_element_type=jnp.float32
    )


def over_blocks(step_fn, running, arrays, size):
    total_rows = arrays[0].shape[0]
    blocks = total_rows // size
    stacked = tuple((item.reshape((blocks, size) + item.shape[1:]) for item in arrays))
    starts = jnp.arange(blocks, dtype=jnp.int32) * size

    def inner(state, element):
        return (step_fn(state, element[0], element[1]), None)

    running, _ = lax.scan(inner, running, (stacked, starts))
    return running


def per_device(
    inputs,
    first_gain,
    first_shift,
    project_weight,
    project_bias,
    attend_weight,
    attend_bias,
    second_gain,
    second_shift,
    expand_weight,
    expand_bias,
    shrink_weight,
    shrink_bias,
    segments,
    block_order,
    cotangent,
):
    own_rows = inputs.shape[1]
    local_width = project_weight.shape[2]
    head_count = local_width // HEAD_DIM
    block_rows = own_rows * lax.axis_size("tensor")
    seq_len = block_rows * lax.axis_size("context")
    half_rows = block_rows // 2
    score_scale = HEAD_DIM ** (-0.5)
    places = stored_places(block_order, half_rows, seq_len)
    seg_stored = jnp.take(segments[0], places)
    my_first = lax.axis_index("context") * block_rows
    query_place = lax.dynamic_slice_in_dim(places, my_first, block_rows)
    query_seg = lax.dynamic_slice_in_dim(seg_stored, my_first, block_rows)
    tokens_own = inputs[0].astype(jnp.float32)
    hidden1 = affine_norm(tokens_own, first_gain, first_shift).astype(jnp.bfloat16)
    hidden1_full = lax.all_gather(hidden1, "tensor", axis=0, tiled=True)
    projected = jnp.einsum(
        "rd,kde->kre", hidden1_full, project_weight, preferred_element_type=jnp.float32
    )
    query_rows = (projected[0] + project_bias[0]).astype(jnp.bfloat16)
    key_rows = projected[1].astype(jnp.bfloat16)
    value_rows = (projected[2] + project_bias[1]).astype(jnp.bfloat16)
    query_heads = split_heads(query_rows)

    def key_mask(key_first, amount):
        key_place = lax.dynamic_slice_in_dim(places, key_first, amount)
        key_seg = lax.dynamic_slice_in_dim(seg_stored, key_first, amount)
        return allowed_pairs(query_place, query_seg, key_place, key_seg)[:, None, :]

    def forward_step(running, pieces, key_first):
        row_max, row_sum, weighted = running
        key_heads = split_heads(pieces[0])
        allowed = key_mask(key_first, pieces[0].shape[0])
        scores = (
            jnp.einsum("qhe,khe->qhk", query_heads, key_heads, preferred_element_type=jnp.float32)
            * score_scale
        )
        scores = jnp.where(allowed, scores, NEG_FILL)
        new_max = jnp.maximum(row_max, jnp.max(scores, axis=-1))
        factor = jnp.exp(row_max - new_max)
        weights = jnp.where(allowed, jnp.exp(scores - new_max[..., None]), 0.0)
        row_sum = row_sum * factor + jnp.sum(weights, axis=-1)
        weighted = weighted * factor[..., None] + jnp.einsum(
            "qhk,khe->qhe",
            weights.astype(jnp.bfloat16),
            split_heads(pieces[1]),
            preferred_element_type=jnp.float32,
        )
        return (new_max, row_sum, weighted)

    start_state = (
        jnp.full((block_rows, head_count), NEG_FILL, jnp.float32),
        jnp.zeros((block_rows, head_count), jnp.float32),
        jnp.zeros((block_rows, head_count, HEAD_DIM), jnp.float32),
    )
    row_max, row_sum, weighted = over_blocks(
        forward_step,
        start_state,
        (
            lax.all_gather(key_rows, "context", axis=0, tiled=True),
            lax.all_gather(value_rows, "context", axis=0, tiled=True),
        ),
        block_rows,
    )
    log_total = row_max + jnp.log(row_sum)
    attended = weighted / row_sum[..., None]
    attended_low = attended.reshape(block_rows, local_width).astype(jnp.bfloat16)
    part = attended_low
    branch = lax.psum_scatter(
        jnp.dot(part, attend_weight, preferred_element_type=jnp.float32).astype(jnp.bfloat16),
        "tensor",
        scatter_dimension=0,
        tiled=True,
    ).astype(jnp.float32)
    middle = tokens_own + branch + attend_bias
    hidden2 = affine_norm(middle, second_gain, second_shift).astype(jnp.bfloat16)
    hidden2_full = lax.all_gather(hidden2, "tensor", axis=0, tiled=True)
    pre_act = jnp.dot(hidden2_full, expand_weight, preferred_element_type=jnp.float32) + expand_bias
    activ = gelu_tanh(pre_act).astype(jnp.bfloat16)
    part = activ
    feed_sum = lax.psum_scatter(
        jnp.dot(part, shrink_weight, preferred_element_type=jnp.float32).astype(jnp.bfloat16),
        "tensor",
        scatter_dimension=0,
        tiled=True,
    ).astype(jnp.float32)
    outputs = (middle + feed_sum + shrink_bias).astype(jnp.bfloat16)[None]
    grad_out = cotangent[0]
    grad_full = lax.all_gather(grad_out, "tensor", axis=0, tiled=True)
    grad_shrink = cross_rows(activ, grad_full)
    grad_shrink_bias = jnp.sum(grad_out.astype(jnp.float32), axis=0)
    grad_act = jnp.dot(grad_full, shrink_weight.T, preferred_element_type=jnp.float32)
    grad_pre = jax.vjp(gelu_tanh, pre_act)[1](grad_act)[0].astype(jnp.bfloat16)
    grad_expand = cross_rows(hidden2_full, grad_pre)
    grad_expand_bias = jnp.sum(grad_pre.astype(jnp.float32), axis=0)
    part = grad_pre
    grad_hidden2 = lax.psum_scatter(
        jnp.dot(part, expand_weight.T, preferred_element_type=jnp.float32).astype(jnp.bfloat16),
        "tensor",
        scatter_dimension=0,
        tiled=True,
    ).astype(jnp.float32)
    second_pull = jax.vjp(affine_norm, middle, second_gain, second_shift)[1]
    grad_middle_norm, grad_second_gain, grad_second_shift = second_pull(grad_hidden2)
    grad_middle = grad_out.astype(jnp.float32) + grad_middle_norm
    grad_middle_low = grad_middle.astype(jnp.bfloat16)
    grad_middle_full = lax.all_gather(grad_middle_low, "tensor", axis=0, tiled=True)
    grad_attend = cross_rows(attended_low, grad_middle_full)
    grad_attend_bias = jnp.sum(grad_middle_low.astype(jnp.float32), axis=0)
    grad_attended = jnp.dot(
        grad_middle_full, attend_weight.T, preferred_element_type=jnp.float32
    ).astype(jnp.bfloat16)
    grad_heads = split_heads(grad_attended)
    delta = jnp.sum(grad_heads.astype(jnp.float32) * attended, axis=-1)

    def probs_for(q_heads, k_heads, lse_rows, allowed):
        scores = (
            jnp.einsum("qhe,khe->qhk", q_heads, k_heads, preferred_element_type=jnp.float32)
            * score_scale
        )
        return jnp.where(allowed, jnp.exp(scores - lse_rows[..., None]), 0.0)

    def grad_scores(weights, out_heads, v_heads, delta_rows):
        grad_weights = jnp.einsum(
            "qhe,khe->qhk", out_heads, v_heads, preferred_element_type=jnp.float32
        )
        return (weights * (grad_weights - delta_rows[..., None])).astype(jnp.bfloat16)

    zero_rows = jnp.zeros((block_rows, head_count, HEAD_DIM), jnp.float32)
    key_all, value_all = (
        lax.all_gather(key_rows, "context", axis=0, tiled=True),
        lax.all_gather(value_rows, "context", axis=0, tiled=True),
    )

    def key_pass(running, key_first):
        key_heads = split_heads(lax.dynamic_slice_in_dim(key_all, key_first, block_rows))
        value_heads = split_heads(lax.dynamic_slice_in_dim(value_all, key_first, block_rows))
        weights = probs_for(query_heads, key_heads, log_total, key_mask(key_first, block_rows))
        score_grad = grad_scores(weights, grad_heads, value_heads, delta)
        running = (
            running
            + jnp.einsum("qhk,khe->qhe", score_grad, key_heads, preferred_element_type=jnp.float32)
            * score_scale
        )
        grad_key = (
            jnp.einsum("qhk,qhe->khe", score_grad, query_heads, preferred_element_type=jnp.float32)
            * score_scale
        )
        grad_value = jnp.einsum(
            "qhk,qhe->khe",
            weights.astype(jnp.bfloat16),
            grad_heads,
            preferred_element_type=jnp.float32,
        )
        return (
            running,
            jnp.concatenate(
                [
                    grad_key.reshape(block_rows, local_width),
                    grad_value.reshape(block_rows, local_width),
                ],
                axis=1,
            ),
        )

    key_starts = jnp.arange(seq_len // block_rows, dtype=jnp.int32) * block_rows
    grad_query, key_terms = lax.scan(key_pass, zero_rows, key_starts)
    key_value_grads = lax.psum_scatter(
        key_terms.reshape(seq_len, 2 * local_width).astype(jnp.bfloat16),
        "context",
        scatter_dimension=0,
        tiled=True,
    ).astype(jnp.float32)
    grad_key = key_value_grads[:, :local_width]
    grad_value = key_value_grads[:, local_width:]
    grad_project_rows = jnp.stack(
        [grad_query.reshape(block_rows, local_width), grad_key, grad_value]
    ).astype(jnp.bfloat16)
    grad_project = jnp.einsum(
        "rd,kre->kde", hidden1_full, grad_project_rows, preferred_element_type=jnp.float32
    )
    grad_project_bias = jnp.stack(
        [
            jnp.sum(grad_project_rows[0].astype(jnp.float32), axis=0),
            jnp.sum(grad_project_rows[2].astype(jnp.float32), axis=0),
        ]
    )
    part = grad_project_rows
    grad_hidden1 = lax.psum_scatter(
        jnp.einsum("kre,kde->rd", part, project_weight, preferred_element_type=jnp.float32).astype(
            jnp.bfloat16
        ),
        "tensor",
        scatter_dimension=0,
        tiled=True,
    ).astype(jnp.float32)
    first_pull = jax.vjp(affine_norm, tokens_own, first_gain, first_shift)[1]
    grad_tokens_norm, grad_first_gain, grad_first_shift = first_pull(grad_hidden1)
    grad_inputs = (grad_middle + grad_tokens_norm).astype(jnp.bfloat16)[None]
    summed = lax.psum(
        (grad_project, grad_project_bias, grad_attend, grad_expand, grad_expand_bias, grad_shrink),
        ("context", "dp"),
    )
    vectors = lax.psum(
        (
            grad_first_gain,
            grad_first_shift,
            grad_attend_bias,
            grad_second_gain,
            grad_second_shift,
            grad_shrink_bias,
        ),
        ("tensor", "context", "dp"),
    )
    return (
        outputs,
        grad_inputs,
        vectors[0],
        vectors[1],
        summed[0],
        summed[1],
        summed[2],
        vectors[2],
        vectors[3],
        vectors[4],
        summed[3],
        summed[4],
        summed[5],
        vectors[5],
    )


def solution(mesh):
    in_specs = (
        P("dp", ("context", "tensor"), None),
        P(),
        P(),
        P(None, None, "tensor"),
        P(None, "tensor"),
        P("tensor", None),
        P(),
        P(),
        P(),
        P(None, "tensor"),
        P("tensor"),
        P("tensor", None),
        P(),
        P("dp", None),
        P(),
        P("dp", ("context", "tensor"), None),
    )
    out_specs = (
        P("dp", ("context", "tensor"), None),
        P("dp", ("context", "tensor"), None),
        P(),
        P(),
        P(None, None, "tensor"),
        P(None, "tensor"),
        P("tensor", None),
        P(),
        P(),
        P(),
        P(None, "tensor"),
        P("tensor"),
        P("tensor", None),
        P(),
    )
    return jax.shard_map(
        per_device, mesh=mesh, in_specs=in_specs, out_specs=out_specs, check_vma=False
    )
```

profile of v0, /device:TPU:0, one launch (start us, length us, event | category | flops | bytes accessed | tf_op | source)
XLA Modules:
  0.0 606.1 jit_solution(4479381773742738639)
XLA Ops:
  10.8 1.9 fusion.54
  12.8 33.1 %all-gather.9.cloned.1.call-done = bf16[768,768]{1,0:T(8,128)(2,1)} async-done(((bf16[192,768]{1,0:T(8,128)(2,1)}), bf16[768,768]{1,0:T(8,128)(2,1)}) %all-gather.9.cloned.1.call-update) | async-done | bytes 1179664 | tf_op jit(solution)/shard_map/all_gather | solution.py:94
  45.9 2.4 fusion.88
  50.5 1.9 fusion.63
  52.7 17.4 %gather_fusion = s32[3072]{0:T(1024)S(1)} fusion(s32[3072]{0:T(1024)S(1)} %bitcast.270, s32[3072]{0:T(1024)S(1)} %broadcast_clamp_fusion), kind=kCustom, calls=%fused_computation | custom fusion | bytes 36864 | tf_op jit(solution)/shard_map/jit(_take)/gather | solution.py:88
  71.5 1.4 dynamic_slice.38
  74.6 3.5 reshape.298
  78.1 1.4 copy.48
  79.5 7.2 %all-gather.11.cloned.1.call-done = bf16[3072,192]{0,1:T(8,128)(2,1)} async-done(((bf16[768,192]{0,1:T(8,128)(2,1)}), bf16[3072,192]{0,1:T(8,128)(2,1)}) %all-gather.11.cloned.1.call-update) | async-done | bytes 1179664 | tf_op jit(solution)/shard_map/all_gather | solution.py:139
  86.7 2.4 copy.58
  89.1 54.7 %while.28 = (s32[]{:T(128)}, f32[768,3]{0,1:T(4,128)S(1)}, f32[768,3]{0,1:T(4,128)}, f32[768,3,64]{0,2,1:T(8,128)S(1)}, s32[768]{0:T(1024)}, /*index=5*/s32[4]{0...) while((s32[]{:T(128)}, f32[768,3]{0,1:T(4,128)S(1)}, ...), condition=%wide.region_6.7_spmd.clone, body=%wide.region_3.6_spmd.clone.sunk | while | flops 478211328 | bytes 27009240 | solution.py:58
  96.0 1.5 fusion.148
  97.5 1.8 fusion.149
  99.9 2.3 fusion.151
  109.2 1.5 fusion.148
  110.7 1.8 fusion.149
  113.8 2.3 fusion.151
  123.0 1.5 fusion.148
  124.6 1.8 fusion.149
  127.7 2.3 fusion.151
  136.9 1.5 fusion.148
  138.4 1.8 fusion.149
  141.5 2.3 fusion.151
  144.6 2.5 convolution_convert_fusion.2
  147.2 29.4 %reduce-scatter.6.cloned.1.call-done = bf16[192,768]{1,0:T(8,128)(2,1)} async-done(((bf16[768,768]{1,0:T(8,128)(2,1)}), bf16[192,768]{1,0:T(8,128)(2,1)}) %reduce-scatter.6.cloned.1.call-update) | async-done | bytes 294928 | tf_op jit(solution)/shard_map/reduce_scatter | solution.py:147
  179.0 1.9 add_convert_fusion.2
  181.8 28.2 %all-gather.13.cloned.1.call-done = bf16[768,768]{1,0:T(8,128)(2,1)} async-done(((bf16[192,768]{1,0:T(8,128)(2,1)}), bf16[768,768]{1,0:T(8,128)(2,1)}) %all-gather.13.cloned.1.call-update) | async-done | bytes 1179664 | tf_op jit(solution)/shard_map/all_gather | solution.py:155
  209.9 4.1 fusion.89
  214.1 26.8 %all-gather.19.cloned.1.call-done = bf16[1,768,768]{2,1,0:T(8,128)(2,1)} async-done(((bf16[1,192,768]{2,1,0:T(8,128)(2,1)}), bf16[1,768,768]{2,1,0:T(8,128)(2,1)}) %all-gather.19.cloned.1.call-update) | async-done | bytes 1179664 | tf_op jit(solution)/shard_map/all_gather | solution.py:167
  240.9 5.0 convert_reduce_fusion
  246.9 2.1 convolution_convert_fusion
  249.2 4.3 convolution_convert_fusion.1
  253.6 24.3 %reduce-scatter.10.cloned.1.call-done = bf16[192,768]{1,0:T(8,128)(2,1)} async-done(((bf16[768,768]{1,0:T(8,128)(2,1)}), bf16[192,768]{1,0:T(8,128)(2,1)}) %reduce-scatter.10.cloned.1.call-update) | async-done | bytes 294928 | tf_op jit(solution)/shard_map/reduce_scatter | solution.py:175
  277.8 1.9 fusion.60
  280.4 28.2 %reduce-scatter.8.cloned.1.call-done = bf16[192,768]{1,0:T(8,128)(2,1)} async-done(((bf16[768,768]{1,0:T(8,128)(2,1)}), bf16[192,768]{1,0:T(8,128)(2,1)}) %reduce-scatter.8.cloned.1.call-update) | async-done | bytes 294928 | tf_op jit(solution)/shard_map/reduce_scatter | solution.py:159
  308.7 2.2 fusion.85
  310.8 1.5 convert_reduce_fusion.5
  313.9 27.4 %all-gather.15.cloned.1.call-done = bf16[768,768]{1,0:T(8,128)(2,1)} async-done(((bf16[192,768]{1,0:T(8,128)(2,1)}), bf16[768,768]{1,0:T(8,128)(2,1)}) %all-gather.15.cloned.1.call-update) | async-done | bytes 1179664 | tf_op jit(solution)/shard_map/all_gather | solution.py:185
  341.4 1.8 convolution_convert_fusion.3
  344.0 62.4 %while.29 = (s32[]{:T(128)}, f32[768,3,64]{0,2,1:T(8,128)S(1)}, bf16[4,768,384]{1,2,0:T(8,128)(2,1)}, s32[4]{0:T(128)}, bf16[3072,192]{0,1:T(8,128)(2,1)}, /*ind...) while((s32[]{:T(128)}, f32[768,3,64]{0,2,1:T(8,128)S(1)}, ...), condition=%wide.region_16.17_spmd.clone, body=%wide.region_15.16_spmd.clone.sunk | while | flops 1153843200 | bytes 39902472 | solution.py:245
  349.9 1.3 constant_dynamic-slice_fusion.7
  352.4 1.7 fusion.165
  354.1 2.7 fusion.163
  368.0 1.7 fusion.165
  369.7 2.7 fusion.163
  383.6 1.7 fusion.165
  385.3 2.7 fusion.163
  399.2 1.7 fusion.165
  400.9 2.7 fusion.163
  406.4 3.4 copy.56
  409.9 32.1 %reduce-scatter.12.cloned.1.call-done = bf16[768,384]{0,1:T(8,128)(2,1)} async-done(((bf16[3072,384]{0,1:T(8,128)(2,1)}), bf16[768,384]{0,1:T(8,128)(2,1)}) %reduce-scatter.12.cloned.1.call-update) | async-done | bytes 589840 | tf_op jit(solution)/shard_map/reduce_scatter | solution.py:246
  443.1 2.3 bitcast_convert_fusion
  445.5 4.3 fusion.91
  449.8 2.8 fusion.37
  453.9 2.1 convolution_bitcast_fusion
  457.2 14.7 %all-reduce.1 = (f32[2,192]{1,0:T(2,128)}, f32[768]{0:T(1024)}) all-reduce(f32[2,192]{1,0:T(2,128)S(1)} %pad_maximum_fusion.3, f32[768]{0:T(1024)S(1)} %copy-done.32), channel_id=1, replica_groups=mesh['tensor'=4,'context'=4,'dp'=2] {'context','dp'}, use_global_device_ids=true, to_apply=%region_28.29 | all-reduce | flops 1152 | bytes 9216 | tf_op jit(solution)/shard_map/psum | solution.py:278
  471.9 3.0 reduce-scatter.14.cloned.1.call-done
  476.2 1.4 fusion.61
  477.5 40.2 %all-reduce = (f32[768]{0:T(1024)}, f32[768]{0:T(1024)}, f32[768]{0:T(1024)}, f32[768]{0:T(1024)}, f32[768]{0:T(1024)}, /*index=5*/f32[768]{0:T(1024)}) all-reduce(f32[768]{0:T(1024)S(1)} %get-tuple-element.278, f32[768]{0:T(1024)S(1)} %get-tuple-element.281, ...), channel_id=1, replica_groups=mesh['tensor'=4,'context'=4,'dp'=2] {'tensor','context','dp'}, use_global_device_ids=true, to_apply=%region_22.23 | all-reduce | flops 4608 | bytes 36864 | tf_op jit(solution)/shard_map/psum | solution.py:282
  517.7 2.0 fusion.69
  519.7 71.8 %all-reduce.5.cloned.1.call-done = (f32[3,768,192]{1,2,0:T(8,128)}, f32[192,768]{1,0:T(8,128)}, f32[768,768]{1,0:T(8,128)}, f32[768,768]{1,0:T(8,128)}) async-done(((f32[3,768,192]{1,2,0:T(8,128)}, f32[192,768]{1,0:T(8,128)}, f32[768,768]{1,0:T(8,128)}, f32[768,768]{1,0:T(8,128)}), (f32[3,768,192]{1,2,0:T(8,128)}, f32[192,768]{1,0:T(8,128)}, f32[768,768]{1,0:T(8,128)}, ...) | async-done | bytes 7077904 | tf_op jit(solution)/shard_map/psum | solution.py:278
  591.5 2.9 copy.85
  595.3 1.4 copy.87
  597.8 1.4 copy.88
  (226 shorter events, 84.3 us)
Async XLA Ops:
  7.2 233.7 %copy-start = (bf16[768,768]{1,0:T(8,128)(2,1)S(1)}, bf16[768,768]{1,0:T(8,128)(2,1)}, u32[]{:S(2)}) copy-start(bf16[768,768]{1,0:T(8,128)(2,1)} %param.31) | copy-start | bytes 3538948
  7.2 38.7 %all-gather.9.cloned.1.call-start = ((), (), s32[]{:S(2)}) async-start(), calls=%async_computation.5 | async-start | bytes 1474560 | tf_op jit(solution)/shard_map/all_gather | solution.py:94
  8.4 1.8 copy-start.16
  9.6 0.6 copy-start.26
  10.2 0.6 copy-start.19
  12.7 61.9 %all-gather.17.cloned.1.call-start = ((), (), s32[]{:S(2)}) async-start(), calls=%async_computation.14 | async-start | bytes 1474560 | tf_op jit(solution)/shard_map/all_gather | solution.py:138
  45.9 4.5 copy-start.33
  45.9 6.6 %copy-start.34 = (s32[8]{0:T(128)S(1)}, s32[8]{0:T(128)}, u32[]{:S(2)}) copy-start(s32[8]{0:T(128)} %param.34) | copy-start | bytes 100
  48.3 1.2 copy-start.10
  48.3 4.3 copy-start.2
  50.3 36.4 %all-gather.11.cloned.1.call-start = ((), (), s32[]{:S(2)}) async-start(), calls=%async_computation.6 | async-start | bytes 1474560 | tf_op jit(solution)/shard_map/all_gather | solution.py:139
  52.4 124.3 %reduce-scatter.6.cloned.1.call-start = ((), (), s32[]{:S(2)}) async-start(), calls=%async_computation.7 | async-start | bytes 1474560 | tf_op jit(solution)/shard_map/reduce_scatter | solution.py:147
  143.8 32.8 %copy-start.3 = (bf16[1,192,768]{2,1,0:T(8,128)(2,1)S(1)}, bf16[1,192,768]{2,1,0:T(8,128)(2,1)}, u32[]{:S(2)}) copy-start(bf16[1,192,768]{2,1,0:T(8,128)(2,1)} %param.20) | copy-start | bytes 884740
  143.8 32.8 %copy-start.13 = (f32[768]{0:T(1024)S(1)}, f32[768]{0:T(1024)}, u32[]{:S(2)}) copy-start(f32[768]{0:T(1024)} %param.26) | copy-start | bytes 9220
  143.8 35.2 %copy-start.15 = (f32[768]{0:T(1024)S(1)}, f32[768]{0:T(1024)}, u32[]{:S(2)}) copy-start(f32[768]{0:T(1024)} %param.27) | copy-start | bytes 9220
  143.8 35.2 %copy-start.31 = (f32[768]{0:T(1024)S(1)}, f32[768]{0:T(1024)}, u32[]{:S(2)}) copy-start(f32[768]{0:T(1024)} %param.28) | copy-start | bytes 9220
  147.2 62.8 %all-gather.13.cloned.1.call-start = ((), (), s32[]{:S(2)}) async-start(), calls=%async_computation.8 | async-start | bytes 1474560 | tf_op jit(solution)/shard_map/all_gather | solution.py:155
  177.8 36.2 %copy-start.18 = (f32[192]{0:T(256)}, f32[192]{0:T(256)S(1)}, u32[]{:S(2)}) copy-start(f32[192]{0:T(256)S(1)} %broadcast_multiply_fusion.1) | copy-start | bytes 2308
  179.0 35.1 %copy-start.28 = (f32[192]{0:T(256)}, f32[192]{0:T(256)S(1)}, u32[]{:S(2)}) copy-start(f32[192]{0:T(256)S(1)} %multiply_reduce_fusion.1) | copy-start | bytes 2308
  179.0 35.0 %copy-start.24 = (f32[192]{0:T(256)}, f32[192]{0:T(256)S(1)}, u32[]{:S(2)}) copy-start(f32[192]{0:T(256)S(1)} %fusion.81) | copy-start | bytes 2308
  180.9 59.9 %all-gather.19.cloned.1.call-start = ((), (), s32[]{:S(2)}) async-start(), calls=%async_computation.15 | async-start | bytes 1474560 | tf_op jit(solution)/shard_map/all_gather | solution.py:167
  181.5 59.4 %copy-start.39 = (f32[768]{0:T(1024)S(1)}, f32[768]{0:T(1024)}, u32[]{:S(2)}) copy-start(f32[768]{0:T(1024)} %param.30) | copy-start | bytes 9220
  181.5 96.3 %reduce-scatter.10.cloned.1.call-start = ((), (), s32[]{:S(2)}) async-start(), calls=%async_computation.10 | async-start | bytes 1474560 | tf_op jit(solution)/shard_map/reduce_scatter | solution.py:175
  240.9 6.1 %copy-start.35 = (bf16[768,768]{1,0:T(8,128)(2,1)S(1)}, bf16[768,768]{1,0:T(8,128)(2,1)}, u32[]{:S(2)}) copy-start(bf16[768,768]{1,0:T(8,128)(2,1)} %param.29) | copy-start | bytes 3538948
  245.9 1.0 copy-start.42
  249.1 28.7 %copy-start.4 = (bf16[192,768]{1,0:T(8,128)(2,1)S(1)}, bf16[192,768]{1,0:T(8,128)(2,1)}, u32[]{:S(2)}) copy-start(bf16[192,768]{1,0:T(8,128)(2,1)} %reduce-scatter.6.cloned.1.call-done) | copy-start | bytes 884740
  249.1 59.6 %reduce-scatter.8.cloned.1.call-start = ((), (), s32[]{:S(2)}) async-start(), calls=%async_computation.9 | async-start | bytes 1474560 | tf_op jit(solution)/shard_map/reduce_scatter | solution.py:159
  253.5 57.4 %copy-start.6 = (bf16[1,192,768]{2,1,0:T(8,128)(2,1)S(1)}, bf16[1,192,768]{2,1,0:T(8,128)(2,1)}, u32[]{:S(2)}) copy-start(bf16[1,192,768]{2,1,0:T(8,128)(2,1)} %param.35) | copy-start | bytes 884740
  253.5 87.8 %copy-start.11 = (bf16[192,768]{1,0:T(8,128)(2,1)S(1)}, bf16[192,768]{1,0:T(8,128)(2,1)}, u32[]{:S(2)}) copy-start(bf16[192,768]{1,0:T(8,128)(2,1)} %param.25) | copy-start | bytes 884740
  253.5 87.8 %all-gather.15.cloned.1.call-start = ((), (), s32[]{:S(2)}) async-start(), calls=%async_computation.11 | async-start | bytes 1474560 | tf_op jit(solution)/shard_map/all_gather | solution.py:185
  310.8 3.1 copy-start.29
  312.3 129.7 %reduce-scatter.12.cloned.1.call-start = ((), (), s32[]{:S(2)}) async-start(), calls=%async_computation.12 | async-start | bytes 2949120 | tf_op jit(solution)/shard_map/reduce_scatter | solution.py:246
  351.3 1.1 copy-start.25
  366.9 1.1 copy-start.25
  382.5 1.1 copy-start.25
  398.0 1.1 copy-start.25
  409.8 33.3 %copy-start.38 = (bf16[3,768,192]{1,2,0:T(8,128)(2,1)S(1)}, bf16[3,768,192]{1,2,0:T(8,128)(2,1)}, u32[]{:S(2)}) copy-start(bf16[3,768,192]{1,2,0:T(8,128)(2,1)} %param.23) | copy-start | bytes 2654212
  409.8 65.0 %reduce-scatter.14.cloned.1.call-start = ((), (), s32[]{:S(2)}) async-start(), calls=%async_computation.13 | async-start | bytes 1474560 | tf_op jit(solution)/shard_map/reduce_scatter | solution.py:267
  445.4 4.4 copy-start.40
  445.4 146.1 %all-reduce.5.cloned.1.call-start = ((), (), s32[]{:S(2)}) async-start(), calls=%async_computation.16 | async-start | bytes 14155776 | tf_op jit(solution)/shard_map/psum | solution.py:278
  445.5 4.3 copy-start.37
  445.5 4.3 copy-start.41
  449.8 2.9 copy-start.5
  449.8 4.1 copy-start.36
  456.0 1.1 copy-start.9
  456.0 1.2 copy-start.32
  456.0 18.9 %copy-start.14 = (f32[768]{0:T(1024)S(1)}, f32[768]{0:T(1024)}, u32[]{:S(2)}) copy-start(f32[768]{0:T(1024)} %param.21) | copy-start | bytes 9220
  456.0 18.9 %copy-start.17 = (f32[192]{0:T(256)S(1)}, f32[192]{0:T(256)}, u32[]{:S(2)}) copy-start(f32[192]{0:T(256)} %copy-done.16) | copy-start | bytes 2308
  456.0 20.1 %copy-start.27 = (f32[192]{0:T(256)S(1)}, f32[192]{0:T(256)}, u32[]{:S(2)}) copy-start(f32[192]{0:T(256)} %copy-done.26) | copy-start | bytes 2308
  456.0 20.2 %copy-start.20 = (f32[192]{0:T(256)S(1)}, f32[192]{0:T(256)}, u32[]{:S(2)}) copy-start(f32[192]{0:T(256)} %copy-done.19) | copy-start | bytes 2308
  456.0 21.5 %copy-start.21 = (f32[768]{0:T(1024)S(1)}, f32[768]{0:T(1024)}, u32[]{:S(2)}) copy-start(f32[768]{0:T(1024)} %get-tuple-element.276) | copy-start | bytes 9220
  456.0 21.5 %copy-start.22 = (f32[768]{0:T(1024)S(1)}, f32[768]{0:T(1024)}, u32[]{:S(2)}) copy-start(f32[768]{0:T(1024)} %get-tuple-element.280) | copy-start | bytes 9220
  456.0 21.5 %copy-start.23 = (f32[768]{0:T(1024)S(1)}, f32[768]{0:T(1024)}, u32[]{:S(2)}) copy-start(f32[768]{0:T(1024)} %get-tuple-element.349) | copy-start | bytes 9220
  456.0 61.7 %copy-start.30 = (f32[192]{0:T(256)S(1)}, f32[192]{0:T(256)}, u32[]{:S(2)}) copy-start(f32[192]{0:T(256)} %copy-done.29) | copy-start | bytes 2308
  591.5 3.0 copy-start.12
  591.5 3.8 copy-start.8
  595.3 2.5 copy-start.7
  595.3 3.9 copy-start.1
Sparse Core Ops, SparseCore 0:
  12.8 32.9 all-gather.8
  50.4 16.6 all-gather.16
  69.2 17.4 all-gather.10
  147.3 29.3 reduce-scatter.5
  181.1 28.8 all-gather.12
  211.4 29.4 all-gather.18
  249.2 28.5 reduce-scatter.9
  280.7 27.9 reduce-scatter.7
  312.5 28.8 all-gather.14
  410.0 32.0 reduce-scatter.11
  445.5 29.3 reduce-scatter.13
  479.6 111.9 all-reduce.4
where the time goes:
time: 609 us; the launch traced here: 606 us
  waiting for transfers between devices  312 us (51%)
  matrix products  80 us (13%)
  local copies, waits for them, and re-layouts  76.5 us (13%)
  blocking collectives  54.9 us (9%)
  other arithmetic  50.8 us (8%)
  loops' own time  16 us (3%)
  between operations  14.8 us (2%)
    psum x1, waiting for transfers between devices, per_device(): lax.psum((grad_project, grad_project_bias, grad_attend, grad_expand, grad...  71.8 us
    psum x1, blocking collectives, per_device(): lax.psum((grad_first_gain, grad_first_shift, grad_attend_bias, grad_secon...  40.2 us
    all_gather x1, waiting for transfers between devices, per_device(): hidden1_full = lax.all_gather(hidden1, 'tensor', axis=0, tiled=True)  33.1 us
    reduce_scatter x1, waiting for transfers between devices, per_device(): lax.psum_scatter(key_terms.reshape(seq_len, 2 * local_width).astype(jnp.b...  32.1 us
    reduce_scatter x1, waiting for transfers between devices, per_device(): lax.psum_scatter(jnp.dot(part, attend_weight, preferred_element_type=jnp....  29.4 us
    reduce_scatter x1, waiting for transfers between devices, per_device(): lax.psum_scatter(jnp.dot(part, shrink_weight, preferred_element_type=jnp....  28.2 us
    all_gather x1, waiting for transfers between devices, per_device(): hidden2_full = lax.all_gather(hidden2, 'tensor', axis=0, tiled=True)  28.2 us
    all_gather x1, waiting for transfers between devices, per_device(): lax.all_gather(grad_middle_low, 'tensor', axis=0, tiled=True)  27.4 us
  transfers between devices with their start and end apart: 12, of which 11 were waited for; matrix products, arithmetic and copies ran while one was open for 9% of the time, Pallas kernels for 0%

commit v1 on v0

--- a/solution.py
+++ b/solution.py
@@ -164,7 +164,24 @@
     ).astype(jnp.float32)
     outputs = (middle + feed_sum + shrink_bias).astype(jnp.bfloat16)[None]
     grad_out = cotangent[0]
-    grad_full = lax.all_gather(grad_out, "tensor", axis=0, tiled=True)
+
+    def run_cube(u):
+        named_axis = "tensor"
+        spare = jax.lax.axis_size(named_axis)
+        u_next, opened = (spare, jax.lax.axis_index(named_axis))
+        f_next, block_now = (u, 1)
+        while block_now < u_next:
+            bank = []
+            for at in range(u_next):
+                bank.append((at, at ^ block_now))
+            v_next = jax.lax.ppermute(f_next, named_axis, bank)
+            field_out = jnp.concatenate([f_next, v_next], 0)
+            main = jnp.concatenate([v_next, f_next], 0)
+            f_next = jnp.where(opened & block_now == 0, field_out, main)
+            block_now = 2 * block_now
+        return f_next
+
+    grad_full = run_cube(grad_out)
     grad_shrink = cross_rows(activ, grad_full)
     grad_shrink_bias = jnp.sum(grad_out.astype(jnp.float32), axis=0)
     grad_act = jnp.dot(grad_full, shrink_weight.T, preferred_element_type=jnp.float32)

time: 609 us -> 597 us (0.980)
  waiting for transfers between devices: 312 us -> 303 us
    all_gather x1 -> x0, waiting for transfers between devices: 26.8 us -> none  [per_device(): grad_full = lax.all_gather(grad_out, 'tensor', axis=0, tiled=True)]
    all_gather x1, waiting for transfers between devices: 28.2 us -> 39.2 us  [per_device(): hidden2_full = lax.all_gather(hidden2, 'tensor', axis=0, tiled=True)]
    ppermute x0 -> x2, waiting for transfers between devices: none -> 9.7 us  [run_cube(): v_next = jax.lax.ppermute(f_next, named_axis, bank)]
    unnamed x89 -> x91, local copies, waits for them, and re-layouts: 13.4 us -> 12.4 us
  transfers between devices with their start and end apart: 12 -> 13, of which waited for: 11 -> 12; matrix products, arithmetic and copies ran while one was open for 9% -> 10% of each run, Pallas kernels for 0% -> 0%
where the time goes in v1:
time: 597 us; the launch traced here: 594 us
  waiting for transfers between devices  303 us (51%)
  matrix products  80.3 us (13%)
  local copies, waits for them, and re-layouts  75.5 us (13%)
  blocking collectives  55.3 us (9%)
  other arithmetic  47.2 us (8%)
  loops' own time  16.2 us (3%)
  between operations  14.5 us (2%)
    psum x1, waiting for transfers between devices, per_device(): lax.psum((grad_project, grad_project_bias, grad_attend, grad_expand, grad...  71.9 us
    psum x1, blocking collectives, per_device(): lax.psum((grad_first_gain, grad_first_shift, grad_attend_bias, grad_secon...  40.3 us
    all_gather x1, waiting for transfers between devices, per_device(): hidden2_full = lax.all_gather(hidden2, 'tensor', axis=0, tiled=True)  39.2 us
    all_gather x1, waiting for transfers between devices, per_device(): hidden1_full = lax.all_gather(hidden1, 'tensor', axis=0, tiled=True)  33.1 us
    reduce_scatter x1, waiting for transfers between devices, per_device(): lax.psum_scatter(key_terms.reshape(seq_len, 2 * local_width).astype(jnp.b...  32 us
    reduce_scatter x1, waiting for transfers between devices, per_device(): lax.psum_scatter(jnp.dot(part, attend_weight, preferred_element_type=jnp....  29.4 us
    reduce_scatter x1, waiting for transfers between devices, per_device(): lax.psum_scatter(jnp.dot(part, shrink_weight, preferred_element_type=jnp....  28.2 us
    all_gather x1, waiting for transfers between devices, per_device(): lax.all_gather(grad_middle_low, 'tensor', axis=0, tiled=True)  27.4 us
  transfers between devices with their start and end apart: 13, of which 12 were waited for; matrix products, arithmetic and copies ran while one was open for 10% of the time, Pallas kernels for 0%

profile of v1, /device:TPU:0, one launch (start us, length us, event | category | flops | bytes accessed | tf_op | source)
XLA Modules:
  0.0 594.1 jit_solution(4764589977020471293)
XLA Ops:
  9.7 1.9 fusion.48
  11.6 33.1 %all-gather.7.cloned.1.call-done = bf16[768,768]{1,0:T(8,128)(2,1)} async-done(((bf16[192,768]{1,0:T(8,128)(2,1)}), bf16[768,768]{1,0:T(8,128)(2,1)}) %all-gather.7.cloned.1.call-update) | async-done | bytes 1179664 | tf_op jit(solution)/shard_map/all_gather | solution.py:94
  44.8 2.4 fusion.85
  49.4 1.9 fusion.56
  51.6 17.4 %gather_fusion = s32[3072]{0:T(1024)S(1)} fusion(s32[3072]{0:T(1024)S(1)} %bitcast.255, s32[3072]{0:T(1024)S(1)} %broadcast_clamp_fusion), kind=kCustom, calls=%fused_computation | custom fusion | bytes 36864 | tf_op jit(solution)/shard_map/jit(_take)/gather | solution.py:88
  70.4 1.4 dynamic_slice.38
  73.5 3.5 reshape.298
  77.0 1.4 copy.48
  78.4 7.2 %all-gather.9.cloned.1.call-done = bf16[3072,192]{0,1:T(8,128)(2,1)} async-done(((bf16[768,192]{0,1:T(8,128)(2,1)}), bf16[3072,192]{0,1:T(8,128)(2,1)}) %all-gather.9.cloned.1.call-update) | async-done | bytes 1179664 | tf_op jit(solution)/shard_map/all_gather | solution.py:139
  85.6 2.4 copy.58
  88.0 50.4 %while.28 = (s32[]{:T(128)}, f32[768,3]{0,1:T(4,128)S(1)}, f32[768,3]{0,1:T(4,128)}, f32[768,3,64]{0,2,1:T(8,128)S(1)}, s32[768]{0:T(1024)}, /*index=5*/s32[4]{0...) while((s32[]{:T(128)}, f32[768,3]{0,1:T(4,128)S(1)}, ...), condition=%wide.region_6.7_spmd.clone, body=%wide.region_3.6_spmd.clone.sunk | while | flops 478211328 | bytes 27083024 | solution.py:58
  94.9 1.5 fusion.145
  96.4 1.8 fusion.146
  98.2 2.3 fusion.148
  107.5 1.5 fusion.145
  109.0 1.8 fusion.146
  110.9 2.3 fusion.148
  120.1 1.5 fusion.145
  121.6 1.8 fusion.146
  123.5 2.3 fusion.148
  132.7 1.5 fusion.145
  134.2 1.8 fusion.146
  136.0 2.3 fusion.148
  139.2 2.5 convolution_convert_fusion.2
  141.8 29.4 %reduce-scatter.6.cloned.1.call-done = bf16[192,768]{1,0:T(8,128)(2,1)} async-done(((bf16[768,768]{1,0:T(8,128)(2,1)}), bf16[192,768]{1,0:T(8,128)(2,1)}) %reduce-scatter.6.cloned.1.call-update) | async-done | bytes 294928 | tf_op jit(solution)/shard_map/reduce_scatter | solution.py:147
  173.6 1.9 add_convert_fusion.2
  175.9 8.3 %collective-permute-done = bf16[192,768]{1,0:T(8,128)(2,1)S(1)} collective-permute-done((bf16[192,768]{1,0:T(8,128)(2,1)S(1)}, bf16[192,768]{1,0:T(8,128)(2,1)S(1)}, u32[]{:S(2)}, u32[]{:S(2)}) %collective-permute-start) | collective-permute-done | bytes 294944 | tf_op jit(solution)/shard_map/ppermute | solution.py:177
  185.2 1.3 collective-permute-start.1
  186.6 39.2 %all-gather.11.cloned.1.call-done = bf16[768,768]{1,0:T(8,128)(2,1)} async-done(((bf16[192,768]{1,0:T(8,128)(2,1)}), bf16[768,768]{1,0:T(8,128)(2,1)}) %all-gather.11.cloned.1.call-update) | async-done | bytes 1179664 | tf_op jit(solution)/shard_map/all_gather | solution.py:155
  225.8 2.7 fusion.86
  228.5 1.4 collective-permute-done.1
  229.9 4.7 convert_reduce_fusion
  235.7 2.1 convolution_convert_fusion
  237.9 4.3 convolution_convert_fusion.1
  242.3 23.9 %reduce-scatter.10.cloned.1.call-done = bf16[192,768]{1,0:T(8,128)(2,1)} async-done(((bf16[768,768]{1,0:T(8,128)(2,1)}), bf16[192,768]{1,0:T(8,128)(2,1)}) %reduce-scatter.10.cloned.1.call-update) | async-done | bytes 294928 | tf_op jit(solution)/shard_map/reduce_scatter | solution.py:192
  266.2 1.9 fusion.53
  268.8 28.2 %reduce-scatter.8.cloned.1.call-done = bf16[192,768]{1,0:T(8,128)(2,1)} async-done(((bf16[768,768]{1,0:T(8,128)(2,1)}), bf16[192,768]{1,0:T(8,128)(2,1)}) %reduce-scatter.8.cloned.1.call-update) | async-done | bytes 294928 | tf_op jit(solution)/shard_map/reduce_scatter | solution.py:159
  297.0 2.2 fusion.82
  299.2 1.5 convert_reduce_fusion.5
  302.3 27.4 %all-gather.13.cloned.1.call-done = bf16[768,768]{1,0:T(8,128)(2,1)} async-done(((bf16[192,768]{1,0:T(8,128)(2,1)}), bf16[768,768]{1,0:T(8,128)(2,1)}) %all-gather.13.cloned.1.call-update) | async-done | bytes 1179664 | tf_op jit(solution)/shard_map/all_gather | solution.py:202
  329.7 1.8 convolution_convert_fusion.3
  332.3 62.4 %while.29 = (s32[]{:T(128)}, f32[768,3,64]{0,2,1:T(8,128)S(1)}, bf16[4,768,384]{1,2,0:T(8,128)(2,1)}, s32[4]{0:T(128)}, bf16[3072,192]{0,1:T(8,128)(2,1)}, /*ind...) while((s32[]{:T(128)}, f32[768,3,64]{0,2,1:T(8,128)S(1)}, ...), condition=%wide.region_16.17_spmd.clone, body=%wide.region_15.16_spmd.clone.sunk | while | flops 1153843200 | bytes 39902472 | solution.py:262
  340.7 1.7 fusion.162
  342.4 2.7 fusion.160
  356.4 1.7 fusion.162
  358.1 2.7 fusion.160
  372.0 1.7 fusion.162
  373.7 2.7 fusion.160
  387.5 1.7 fusion.162
  389.2 2.7 fusion.160
  394.7 3.4 copy.56
  398.2 32.0 %reduce-scatter.12.cloned.1.call-done = bf16[768,384]{0,1:T(8,128)(2,1)} async-done(((bf16[3072,384]{0,1:T(8,128)(2,1)}), bf16[768,384]{0,1:T(8,128)(2,1)}) %reduce-scatter.12.cloned.1.call-update) | async-done | bytes 589840 | tf_op jit(solution)/shard_map/reduce_scatter | solution.py:263
  431.4 2.2 bitcast_convert_fusion
  433.6 4.3 fusion.88
  438.0 4.9 fusion.64
  444.1 2.1 convolution_bitcast_fusion
  447.4 15.0 %all-reduce.1 = (f32[2,192]{1,0:T(2,128)}, f32[768]{0:T(1024)}) all-reduce(f32[2,192]{1,0:T(2,128)S(1)} %pad_maximum_fusion.3, f32[768]{0:T(1024)S(1)} %copy-done.35), channel_id=1, replica_groups=mesh['tensor'=4,'context'=4,'dp'=2] {'context','dp'}, use_global_device_ids=true, to_apply=%region_28.29 | all-reduce | flops 1152 | bytes 9216 | tf_op jit(solution)/shard_map/psum | solution.py:295
  464.3 1.4 fusion.54
  465.7 40.3 %all-reduce = (f32[768]{0:T(1024)}, f32[768]{0:T(1024)}, f32[768]{0:T(1024)}, f32[768]{0:T(1024)}, f32[768]{0:T(1024)}, /*index=5*/f32[768]{0:T(1024)}) all-reduce(f32[768]{0:T(1024)S(1)} %get-tuple-element.278, f32[768]{0:T(1024)S(1)} %get-tuple-element.281, ...), channel_id=1, replica_groups=mesh['tensor'=4,'context'=4,'dp'=2] {'tensor','context','dp'}, use_global_device_ids=true, to_apply=%region_22.23 | all-reduce | flops 4608 | bytes 36864 | tf_op jit(solution)/shard_map/psum | solution.py:299
  506.0 2.0 fusion.62
  508.0 71.9 %all-reduce.5.cloned.1.call-done = (f32[3,768,192]{1,2,0:T(8,128)}, f32[192,768]{1,0:T(8,128)}, f32[768,768]{1,0:T(8,128)}, f32[768,768]{1,0:T(8,128)}) async-done(((f32[3,768,192]{1,2,0:T(8,128)}, f32[192,768]{1,0:T(8,128)}, f32[768,768]{1,0:T(8,128)}, f32[768,768]{1,0:T(8,128)}), (f32[3,768,192]{1,2,0:T(8,128)}, f32[192,768]{1,0:T(8,128)}, f32[768,768]{1,0:T(8,128)}, ...) | async-done | bytes 7077904 | tf_op jit(solution)/shard_map/psum | solution.py:295
  579.9 2.9 copy.85
  583.7 1.4 copy.87
  586.2 1.4 copy.88
  (245 shorter events, 81.2 us)
Async XLA Ops:
  7.2 222.7 %copy-start = (bf16[768,768]{1,0:T(8,128)(2,1)S(1)}, bf16[768,768]{1,0:T(8,128)(2,1)}, u32[]{:S(2)}) copy-start(bf16[768,768]{1,0:T(8,128)(2,1)} %param.31) | copy-start | bytes 3538948
  7.2 37.5 %all-gather.7.cloned.1.call-start = ((), (), s32[]{:S(2)}) async-start(), calls=%async_computation.5 | async-start | bytes 1474560 | tf_op jit(solution)/shard_map/all_gather | solution.py:94
  8.4 36.3 %copy-start.18 = (f32[192]{0:T(256)}, f32[192]{0:T(256)S(1)}, u32[]{:S(2)}) copy-start(f32[192]{0:T(256)S(1)} %broadcast_multiply_fusion.2) | copy-start | bytes 2308
  9.6 35.1 %copy-start.29 = (f32[192]{0:T(256)}, f32[192]{0:T(256)S(1)}, u32[]{:S(2)}) copy-start(f32[192]{0:T(256)S(1)} %fusion.50) | copy-start | bytes 2308
  9.6 35.1 %copy-start.21 = (f32[192]{0:T(256)}, f32[192]{0:T(256)S(1)}, u32[]{:S(2)}) copy-start(f32[192]{0:T(256)S(1)} %fusion.75) | copy-start | bytes 2308
  11.6 61.9 %all-gather.15.cloned.1.call-start = ((), (), s32[]{:S(2)}) async-start(), calls=%async_computation.14 | async-start | bytes 1474560 | tf_op jit(solution)/shard_map/all_gather | solution.py:138
  44.8 4.5 copy-start.36
  44.8 6.6 %copy-start.37 = (s32[8]{0:T(128)S(1)}, s32[8]{0:T(128)}, u32[]{:S(2)}) copy-start(s32[8]{0:T(128)} %param.34) | copy-start | bytes 100
  47.2 1.2 copy-start.10
  47.2 4.3 copy-start.2
  49.2 36.4 %all-gather.9.cloned.1.call-start = ((), (), s32[]{:S(2)}) async-start(), calls=%async_computation.6 | async-start | bytes 1474560 | tf_op jit(solution)/shard_map/all_gather | solution.py:139
  51.3 119.9 %reduce-scatter.6.cloned.1.call-start = ((), (), s32[]{:S(2)}) async-start(), calls=%async_computation.7 | async-start | bytes 1474560 | tf_op jit(solution)/shard_map/reduce_scatter | solution.py:147
  96.4 1.8 copy-start.12
  98.2 2.3 copy-start.13
  109.0 1.8 copy-start.12
  110.8 2.3 copy-start.13
  121.6 1.8 copy-start.12
  123.5 2.3 copy-start.13
  134.2 1.8 copy-start.12
  136.0 2.3 copy-start.13
  138.3 32.9 %copy-start.3 = (bf16[1,192,768]{2,1,0:T(8,128)(2,1)S(1)}, bf16[1,192,768]{2,1,0:T(8,128)(2,1)}, u32[]{:S(2)}) copy-start(bf16[1,192,768]{2,1,0:T(8,128)(2,1)} %param.20) | copy-start | bytes 884740
  138.4 32.9 %copy-start.15 = (f32[768]{0:T(1024)S(1)}, f32[768]{0:T(1024)}, u32[]{:S(2)}) copy-start(f32[768]{0:T(1024)} %param.26) | copy-start | bytes 9220
  138.4 35.2 %copy-start.17 = (f32[768]{0:T(1024)S(1)}, f32[768]{0:T(1024)}, u32[]{:S(2)}) copy-start(f32[768]{0:T(1024)} %param.27) | copy-start | bytes 9220
  138.4 35.2 %copy-start.34 = (f32[768]{0:T(1024)S(1)}, f32[768]{0:T(1024)}, u32[]{:S(2)}) copy-start(f32[768]{0:T(1024)} %param.28) | copy-start | bytes 9220
  139.2 36.6 %copy-start.6 = (bf16[1,192,768]{2,1,0:T(8,128)(2,1)S(1)}, bf16[1,192,768]{2,1,0:T(8,128)(2,1)}, u32[]{:S(2)}) copy-start(bf16[1,192,768]{2,1,0:T(8,128)(2,1)} %param.35) | copy-start | bytes 884740
  141.8 84.0 %all-gather.11.cloned.1.call-start = ((), (), s32[]{:S(2)}) async-start(), calls=%async_computation.8 | async-start | bytes 1474560 | tf_op jit(solution)/shard_map/all_gather | solution.py:155
  172.4 3.4 copy-start.20
  173.6 2.2 copy-start.31
  173.6 2.1 copy-start.27
  175.5 90.6 %reduce-scatter.10.cloned.1.call-start = ((), (), s32[]{:S(2)}) async-start(), calls=%async_computation.10 | async-start | bytes 1474560 | tf_op jit(solution)/shard_map/reduce_scatter | solution.py:192
  175.8 8.4 %collective-permute-start = (bf16[192,768]{1,0:T(8,128)(2,1)S(1)}, bf16[192,768]{1,0:T(8,128)(2,1)S(1)}, u32[]{:S(2)}, u32[]{:S(2)}) collective-permute-start(bf16[192,768]{1,0:T(8,128)(2,1)S(1)} %bitcast.269), channel_id=1, source_target_pairs={{0,8},{8,0},{16,24},{24,16},{1,9},{9,1},{17,25},{25,17},{2,10},{10... | collective-permute-start | bytes 884744 | tf_op jit(solution)/shard_map/ppermute | solution.py:177
  185.2 44.7 %collective-permute-start.1 = (bf16[384,768]{1,0:T(8,128)(2,1)}, bf16[384,768]{1,0:T(8,128)(2,1)}, u32[]{:S(2)}, u32[]{:S(2)}) collective-permute-start(bf16[384,768]{1,0:T(8,128)(2,1)} %maximum_select_fusion.1), channel_id=1, source_target_pairs={{0,16},{8,24},{16,0},{24,8},{1,17},{9,25},{17,1},{25,9},{2,18},{10... | collective-permute-start | bytes 1769480 | tf_op jit(solution)/shard_map/ppermute | solution.py:177
  186.6 43.3 %copy-start.41 = (f32[768]{0:T(1024)S(1)}, f32[768]{0:T(1024)}, u32[]{:S(2)}) copy-start(f32[768]{0:T(1024)} %param.30) | copy-start | bytes 9220
  228.5 6.1 %copy-start.43 = (f32[768,768]{1,0:T(8,128)}, f32[768,768]{1,0:T(8,128)S(1)}, u32[]{:S(2)}) copy-start(f32[768,768]{1,0:T(8,128)S(1)} %fusion.86) | copy-start | bytes 7077892
  228.5 7.1 %copy-start.38 = (bf16[768,768]{1,0:T(8,128)(2,1)S(1)}, bf16[768,768]{1,0:T(8,128)(2,1)}, u32[]{:S(2)}) copy-start(bf16[768,768]{1,0:T(8,128)(2,1)} %param.29) | copy-start | bytes 3538948
  237.8 28.3 %copy-start.4 = (bf16[192,768]{1,0:T(8,128)(2,1)S(1)}, bf16[192,768]{1,0:T(8,128)(2,1)}, u32[]{:S(2)}) copy-start(bf16[192,768]{1,0:T(8,128)(2,1)} %reduce-scatter.6.cloned.1.call-done) | copy-start | bytes 884740
  237.8 59.2 %reduce-scatter.8.cloned.1.call-start = ((), (), s32[]{:S(2)}) async-start(), calls=%async_computation.9 | async-start | bytes 1474560 | tf_op jit(solution)/shard_map/reduce_scatter | solution.py:159
  242.2 87.5 %copy-start.11 = (bf16[192,768]{1,0:T(8,128)(2,1)S(1)}, bf16[192,768]{1,0:T(8,128)(2,1)}, u32[]{:S(2)}) copy-start(bf16[192,768]{1,0:T(8,128)(2,1)} %param.25) | copy-start | bytes 884740
  242.2 87.4 %all-gather.13.cloned.1.call-start = ((), (), s32[]{:S(2)}) async-start(), calls=%async_computation.11 | async-start | bytes 1474560 | tf_op jit(solution)/shard_map/all_gather | solution.py:202
  299.2 1.8 copy-start.32
  300.7 129.6 %reduce-scatter.12.cloned.1.call-start = ((), (), s32[]{:S(2)}) async-start(), calls=%async_computation.12 | async-start | bytes 2949120 | tf_op jit(solution)/shard_map/reduce_scatter | solution.py:263
  339.6 1.1 copy-start.28
  386.4 1.1 copy-start.28
  398.1 33.2 %copy-start.40 = (bf16[3,768,192]{1,2,0:T(8,128)(2,1)S(1)}, bf16[3,768,192]{1,2,0:T(8,128)(2,1)}, u32[]{:S(2)}) copy-start(bf16[3,768,192]{1,2,0:T(8,128)(2,1)} %param.23) | copy-start | bytes 2654212
  398.1 64.9 %reduce-scatter.14.cloned.1.call-start = ((), (), s32[]{:S(2)}) async-start(), calls=%async_computation.13 | async-start | bytes 1474560 | tf_op jit(solution)/shard_map/reduce_scatter | solution.py:284
  433.6 4.4 copy-start.42
  433.6 146.3 %all-reduce.5.cloned.1.call-start = ((), (), s32[]{:S(2)}) async-start(), calls=%async_computation.15 | async-start | bytes 14155776 | tf_op jit(solution)/shard_map/psum | solution.py:295
  433.6 4.3 copy-start.44
  438.0 4.9 copy-start.5
  438.0 6.1 %copy-start.39 = (bf16[768,768]{1,0:T(8,128)(2,1)S(1)}, bf16[768,768]{1,0:T(8,128)(2,1)}, u32[]{:S(2)}) copy-start(bf16[768,768]{1,0:T(8,128)(2,1)} %all-gather.7.cloned.1.call-done) | copy-start | bytes 3538948
  446.2 1.2 copy-start.35
  446.2 16.9 %copy-start.16 = (f32[768]{0:T(1024)S(1)}, f32[768]{0:T(1024)}, u32[]{:S(2)}) copy-start(f32[768]{0:T(1024)} %param.21) | copy-start | bytes 9220
  446.2 16.9 %copy-start.19 = (f32[192]{0:T(256)S(1)}, f32[192]{0:T(256)}, u32[]{:S(2)}) copy-start(f32[192]{0:T(256)} %copy-done.18) | copy-start | bytes 2308
  446.2 18.1 %copy-start.30 = (f32[192]{0:T(256)S(1)}, f32[192]{0:T(256)}, u32[]{:S(2)}) copy-start(f32[192]{0:T(256)} %copy-done.29) | copy-start | bytes 2308
  446.2 18.1 %copy-start.22 = (f32[192]{0:T(256)S(1)}, f32[192]{0:T(256)}, u32[]{:S(2)}) copy-start(f32[192]{0:T(256)} %copy-done.21) | copy-start | bytes 2308
  446.2 19.5 %copy-start.23 = (f32[768]{0:T(1024)S(1)}, f32[768]{0:T(1024)}, u32[]{:S(2)}) copy-start(f32[768]{0:T(1024)} %get-tuple-element.276) | copy-start | bytes 9220
  446.2 19.5 %copy-start.24 = (f32[768]{0:T(1024)S(1)}, f32[768]{0:T(1024)}, u32[]{:S(2)}) copy-start(f32[768]{0:T(1024)} %get-tuple-element.280) | copy-start | bytes 9220
  446.2 19.5 %copy-start.25 = (f32[768]{0:T(1024)S(1)}, f32[768]{0:T(1024)}, u32[]{:S(2)}) copy-start(f32[768]{0:T(1024)} %get-tuple-element.349) | copy-start | bytes 9220
  446.2 19.5 %copy-start.26 = (f32[768]{0:T(1024)S(1)}, f32[768]{0:T(1024)}, u32[]{:S(2)}) copy-start(f32[768]{0:T(1024)} %get-tuple-element.362) | copy-start | bytes 9220
  446.3 59.8 %copy-start.33 = (f32[192]{0:T(256)S(1)}, f32[192]{0:T(256)}, u32[]{:S(2)}) copy-start(f32[192]{0:T(256)} %copy-done.32) | copy-start | bytes 2308
  579.9 3.0 copy-start.14
  579.9 3.8 copy-start.8
  583.7 2.5 copy-start.7
  583.7 3.9 copy-start.1
  (4 other events, 4.4 us)
Sparse Core Ops, SparseCore 0:
  11.7 32.9 all-gather.6
  49.3 16.6 all-gather.14
  68.1 17.4 all-gather.8
  141.9 29.3 reduce-scatter.5
  175.6 50.1 all-gather.10
  237.9 28.1 reduce-scatter.9
  269.0 27.9 reduce-scatter.7
  300.8 28.8 all-gather.12
  398.3 31.9 reduce-scatter.11
  433.7 29.3 reduce-scatter.13
  467.9 111.9 all-reduce.4
